TPU v7x, 32 devices: a whole 2x2x4 slice. The times are simulated.
32 devices in a mesh: dp: 4 (over x, core), row: 4 (over z), col: 2 (over y).
Axes of the slice: x: 2, y: 2, z: 4, core: 2. Of those that a mesh axis runs over, the one named last changes fastest.
Arguments:
- tokens: bfloat16 [4096, 4096], P(('dp', 'col'), 'row'), may hold values from -6 to 6
- cotangent: bfloat16 [4096, 4096], P(('dp', 'col'), 'row'), may hold values from -6 to 6
- gate_pre: bfloat16 [4096, 14336], P(('dp', 'row'), 'col'), may hold values from -6 to 6
- up_pre: bfloat16 [4096, 14336], P(('dp', 'row'), 'col'), may hold values from -6 to 6
- w_gate: bfloat16 [14336, 4096], P('col', 'row'), may hold values from -0.09375 to 0.09375
- w_up: bfloat16 [14336, 4096], P('col', 'row'), may hold values from -0.09375 to 0.09375
- w_down: bfloat16 [4096, 14336], P('row', 'col'), may hold values from -0.046875 to 0.046875
Outputs:
- d_tokens: bfloat16 [4096, 4096], P(('dp', 'col'), 'row')
- grad_gate: float32 [14336, 4096], P(('col', 'dp'), 'row')
- grad_up: float32 [14336, 4096], P(('col', 'dp'), 'row')
- grad_down: float32 [4096, 14336], P(('row', 'dp'), 'col')
All inputs are finite; a program needn't handle non-finite values.
Results may differ from a plain program's by a relative error of at most 0.02.
Values may be sent and summed in bfloat16 or wider, within the bound.
A program may use at most 256 MiB of HBM per device.

v0:
```python
import jax
import jax.numpy as jnp
from jax import lax
from jax.sharding import PartitionSpec as P


def contract_tokens(left, right):
    return lax.dot_general(
        left, right, (((0,), (0,)), ((), ())), preferred_element_type=jnp.float32
    )


def local_grads(hidden_grad, gate_pre, up_pre):
    gate_value = gate_pre.astype(jnp.float32)
    up_value = up_pre.astype(jnp.float32)
    sigmoid_gate = jax.nn.sigmoid(gate_value)
    hidden = (gate_value * sigmoid_gate * up_value).astype(jnp.bfloat16)
    gate_grad = (
        hidden_grad * up_value * sigmoid_gate * (1.0 + gate_value * (1.0 - sigmoid_gate))
    ).astype(jnp.bfloat16)
    up_grad = (hidden_grad * gate_value * sigmoid_gate).astype(jnp.bfloat16)
    return (hidden, gate_grad, up_grad)


def local(tokens, cotangent, gate_pre, up_pre, w_gate, w_up, w_down):
    tok_cols, cot_cols = (
        lax.all_gather(tokens, "col", axis=0, tiled=True),
        lax.all_gather(cotangent, "col", axis=0, tiled=True),
    )
    partial_grad = jnp.dot(cot_cols, w_down, preferred_element_type=jnp.float32)
    hidden_grad = lax.psum(partial_grad.astype(jnp.bfloat16), "row").astype(jnp.float32)
    gate_all, up_all = (
        lax.all_gather(gate_pre, "row", axis=0, tiled=True),
        lax.all_gather(up_pre, "row", axis=0, tiled=True),
    )
    hidden, gate_grad, up_grad = local_grads(hidden_grad, gate_all, up_all)
    d_tokens = lax.psum_scatter(
        (
            jnp.dot(gate_grad, w_gate, preferred_element_type=jnp.float32)
            + jnp.dot(up_grad, w_up, preferred_element_type=jnp.float32)
        ).astype(jnp.bfloat16),
        "col",
        scatter_dimension=0,
        tiled=True,
    )
    grad_down = lax.psum_scatter(
        contract_tokens(cot_cols, hidden).astype(jnp.bfloat16),
        "dp",
        scatter_dimension=0,
        tiled=True,
    ).astype(jnp.float32)
    feature_count = w_gate.shape[1]
    stacked = lax.psum_scatter(
        jnp.concatenate(
            [contract_tokens(gate_grad, tok_cols), contract_tokens(up_grad, tok_cols)], axis=1
        ).astype(jnp.bfloat16),
        "dp",
        scatter_dimension=0,
        tiled=True,
    ).astype(jnp.float32)
    grad_gate = stacked[:, :feature_count]
    grad_up = stacked[:, feature_count:]
    return (d_tokens, grad_gate, grad_up, grad_down)


def solution(mesh):
    placed = (
        P(("dp", "col"), "row"),
        P(("dp", "col"), "row"),
        P(("dp", "row"), "col"),
        P(("dp", "row"), "col"),
        P("col", "row"),
        P("col", "row"),
        P("row", "col"),
    )
    return jax.shard_map(
        local,
        mesh=mesh,
        in_specs=placed,
        out_specs=(
            P(("dp", "col"), "row"),
            P(("col", "dp"), "row"),
            P(("col", "dp"), "row"),
            P(("row", "dp"), "col"),
        ),
        check_vma=False,
    )
```

profile of v0, /device:TPU:0, one launch (start us, length us, event | category | flops | bytes accessed | tf_op | source)
XLA Modules:
  0.0 1437.2 jit_solution(5142862341557165757)
XLA Ops:
  7.2 0.7 all-gather.5.cloned.1.call-update
  7.9 0.7 all-gather.9.cloned.1.call-update
  8.7 0.7 all-gather.7.cloned.1.call-update
  9.4 35.9 %all-gather.5.cloned.1.call-done = bf16[1024,1024]{1,0:T(8,128)(2,1)} async-done(((bf16[512,1024]{1,0:T(8,128)(2,1)}), bf16[1024,1024]{1,0:T(8,128)(2,1)}) %all-gather.5.cloned.1.call-update) | async-done | bytes 2097168 | tf_op jit(solution)/shard_map/all_gather | solution.py:28
  45.4 22.2 %convolution_convert_fusion.2 = bf16[1024,7168]{1,0:T(8,128)(2,1)} fusion(bf16[1024,1024]{1,0:T(8,128)(2,1)} %all-gather.5.cloned.1.call-done, bf16[1024,7168]{1,0:T(8,128)(2,1)} %param.13), kind=kOutput, calls=%fused_computation.21 | convolution fusion | flops 15039725568 | bytes 31457280 | tf_op jit(solution)/shard_map/dot_general | solution.py:30
  67.7 0.5 all-gather.11.cloned.1.call-update
  68.2 231.2 %all-gather.9.cloned.1.call-done = bf16[1024,7168]{1,0:T(8,128)(2,1)} async-done(((bf16[256,7168]{1,0:T(8,128)(2,1)}), bf16[1024,7168]{1,0:T(8,128)(2,1)}) %all-gather.9.cloned.1.call-update) | async-done | bytes 14680080 | tf_op jit(solution)/shard_map/all_gather | solution.py:33
  299.4 252.3 %all-gather.7.cloned.1.call-done = bf16[1024,7168]{1,0:T(8,128)(2,1)} async-done(((bf16[256,7168]{1,0:T(8,128)(2,1)}), bf16[1024,7168]{1,0:T(8,128)(2,1)}) %all-gather.7.cloned.1.call-update) | async-done | bytes 14680080 | tf_op jit(solution)/shard_map/all_gather | solution.py:34
  551.7 26.8 %convert_bitcast_fusion = bf16[1024,7168]{0,1:T(8,128)(2,1)} fusion(bf16[1024,1024]{1,0:T(8,128)(2,1)S(1)} %copy-done, bf16[1024,7168]{1,0:T(8,128)(2,1)} %all-gather.7.cloned.1.call-done, bf16[1024,7168]{1,0:T(8,128)(2,1)} %all-gather.9.cloned.1.call-done), kind=kOutput, calls=%fused_computation.17 | convolution fusion | flops 15098445824 | bytes 46137344 | tf_op jit(solution)/shard_map/dot_general | solution.py:8
  578.7 467.3 %all-reduce.2.cloned.1.call-done = bf16[1024,7168]{1,0:T(8,128)(2,1)} async-done(((bf16[1024,7168]{1,0:T(8,128)(2,1)}), bf16[1024,7168]{1,0:T(8,128)(2,1)}) %all-reduce.2.cloned.1.call-update) | async-done | bytes 14680080 | tf_op jit(solution)/shard_map/psum | solution.py:31
  1046.0 31.7 %fusion.9 = (bf16[1024,7168]{1,0:T(8,128)(2,1)}, bf16[1024,7168]{1,0:T(8,128)(2,1)}) fusion(bf16[1024,7168]{1,0:T(8,128)(2,1)} %all-gather.9.cloned.1.call-done, bf16[1024,7168]{1,0:T(8,128)(2,1)} %all-reduce.2.cloned.1.call-done, bf16[1024,7168]{1,0:T(8,128)(2,1)} %all-gather.7.cloned.1.call-done), kind=kLoop, calls=%fused_computation.15 | loop fusion | flops 117440512 | bytes 73400320 | tf_op jit(solution)/shard_map/convert_element_type | solution.py:21
  1077.7 1.6 all-gather.11.cloned.1.call-done
  1079.4 24.4 %convolution_convert_fusion = bf16[7168,1024]{0,1:T(8,128)(2,1)} fusion(bf16[1024,7168]{1,0:T(8,128)(2,1)} %get-tuple-element.8, bf16[1024,1024]{1,0:T(8,128)(2,1)} %all-gather.11.cloned.1.call-done), kind=kOutput, calls=%fused_computation.19 | convolution fusion | flops 15039725568 | bytes 31457280 | tf_op jit(solution)/shard_map/dot_general | solution.py:8
  1103.8 23.4 %convolution_convert_fusion.1 = bf16[7168,1024]{0,1:T(8,128)(2,1)} fusion(bf16[1024,7168]{1,0:T(8,128)(2,1)} %get-tuple-element.9, bf16[1024,1024]{1,0:T(8,128)(2,1)S(1)} %copy-done.1), kind=kOutput, calls=%fused_computation.20 | convolution fusion | flops 15039725568 | bytes 31457280 | tf_op jit(solution)/shard_map/dot_general | solution.py:8
  1127.2 21.4 %pad_maximum_fusion = bf16[7168,2048]{0,1:T(8,128)(2,1)} fusion(bf16[7168,1024]{0,1:T(8,128)(2,1)} %convolution_convert_fusion, bf16[7168,1024]{0,1:T(8,128)(2,1)} %convolution_convert_fusion.1), kind=kLoop, calls=%fused_computation.16 | loop fusion | flops 58720256 | bytes 58720256 | tf_op jit(solution)/shard_map/concatenate | solution.py:54
  1148.7 19.2 %fusion.16 = f32[1024,1024]{1,0:T(8,128)S(1)} fusion(bf16[1024,7168]{1,0:T(8,128)(2,1)} %get-tuple-element.9, bf16[7168,1024]{1,0:T(8,128)(2,1)} %param.11), kind=kOutput, calls=%fused_computation.25 | convolution fusion | flops 15032385536 | bytes 33554432 | tf_op jit(solution)/shard_map/dot_general | solution.py:39
  1167.9 21.0 %add_convert_fusion = bf16[1024,1024]{1,0:T(8,128)(2,1)} fusion(f32[1024,1024]{1,0:T(8,128)S(1)} %fusion.16, bf16[1024,7168]{1,0:T(8,128)(2,1)} %get-tuple-element.8, bf16[7168,1024]{1,0:T(8,128)(2,1)} %param.12), kind=kOutput, calls=%fused_computation.22 | convolution fusion | flops 15034482688 | bytes 35651584 | tf_op jit(solution)/shard_map/dot_general | solution.py:40
  1189.0 2.9 reduce-scatter.8.cloned.1.call-done
  1191.9 6.1 copy.13
  1198.1 197.5 %reduce-scatter.6.cloned.1.call-done = bf16[1792,2048]{0,1:T(8,128)(2,1)} async-done(((bf16[7168,2048]{0,1:T(8,128)(2,1)}), bf16[1792,2048]{0,1:T(8,128)(2,1)}) %reduce-scatter.6.cloned.1.call-update) | async-done | bytes 7340048 | tf_op jit(solution)/shard_map/reduce_scatter | solution.py:53
  1395.6 9.7 fusion.15
  1405.2 8.4 copy.12
  1413.6 8.4 copy.11
  1422.0 8.3 reduce-scatter.4.cloned.1.call-done
  (16 shorter events, 0.6 us)
Async XLA Ops:
  7.2 38.2 %all-gather.5.cloned.1.call-start = ((), (), s32[]{:S(2)}) async-start(), calls=%async_computation.3 | async-start | bytes 3145728 | tf_op jit(solution)/shard_map/all_gather | solution.py:28
  7.9 291.5 %all-gather.9.cloned.1.call-start = ((), (), s32[]{:S(2)}) async-start(), calls=%async_computation.6 | async-start | bytes 18350080 | tf_op jit(solution)/shard_map/all_gather | solution.py:33
  8.6 543.0 %all-gather.7.cloned.1.call-start = ((), (), s32[]{:S(2)}) async-start(), calls=%async_computation.5 | async-start | bytes 18350080 | tf_op jit(solution)/shard_map/all_gather | solution.py:34
  9.4 1036.6 %all-reduce.2.cloned.1.call-start = ((), (), s32[]{:S(2)}) async-start(), calls=%async_computation.4 | async-start | bytes 29360128 | tf_op jit(solution)/shard_map/psum | solution.py:31
  67.6 484.1 %copy-start = (bf16[1024,1024]{1,0:T(8,128)(2,1)S(1)}, bf16[1024,1024]{1,0:T(8,128)(2,1)}, u32[]{:S(2)}) copy-start(bf16[1024,1024]{1,0:T(8,128)(2,1)} %all-gather.5.cloned.1.call-done) | copy-start | bytes 6291460
  67.6 1011.8 %all-gather.11.cloned.1.call-start = ((), (), s32[]{:S(2)}) async-start(), calls=%async_computation.8 | async-start | bytes 3145728 | tf_op jit(solution)/shard_map/all_gather | solution.py:27
  68.2 1123.7 %reduce-scatter.8.cloned.1.call-start = ((), (), s32[]{:S(2)}) async-start(), calls=%async_computation.10 | async-start | bytes 18350080 | tf_op jit(solution)/shard_map/reduce_scatter | solution.py:46
  578.5 817.1 %reduce-scatter.6.cloned.1.call-start = ((), (), s32[]{:S(2)}) async-start(), calls=%async_computation.9 | async-start | bytes 36700160 | tf_op jit(solution)/shard_map/reduce_scatter | solution.py:53
  1079.4 24.4 %copy-start.1 = (bf16[1024,1024]{1,0:T(8,128)(2,1)S(1)}, bf16[1024,1024]{1,0:T(8,128)(2,1)}, u32[]{:S(2)}) copy-start(bf16[1024,1024]{1,0:T(8,128)(2,1)} %all-gather.11.cloned.1.call-done) | copy-start | bytes 6291460
  1148.7 281.7 %reduce-scatter.4.cloned.1.call-start = ((), (), s32[]{:S(2)}) async-start(), calls=%async_computation.7 | async-start | bytes 3145728 | tf_op jit(solution)/shard_map/reduce_scatter | solution.py:37
Sparse Core Ops, SparseCore 0:
  9.5 35.8 all-gather.4
  46.9 252.4 all-gather.8
  301.0 250.6 all-gather.6
  554.0 491.9 all-reduce.1
  1047.4 31.9 all-gather.10
  1081.8 110.0 reduce-scatter.7
  1194.5 201.0 reduce-scatter.5
  1398.4 31.8 reduce-scatter.3
where the time goes:
time: 1440 us
  waiting for transfers between devices  1200 us (83%)
  matrix products  137 us (10%)
  other arithmetic  53.2 us (4%)
  local copies, waits for them, and re-layouts  32.6 us (2%)
    psum x1, waiting for transfers between devices, local(): lax.psum(partial_grad.astype(jnp.bfloat16), 'row').astype(jnp.float32)  467 us
    all_gather x1, waiting for transfers between devices, local(): lax.all_gather(up_pre, 'row', axis=0, tiled=True)  252 us
    all_gather x1, waiting for transfers between devices, local(): lax.all_gather(gate_pre, 'row', axis=0, tiled=True)  231 us
    reduce_scatter x1, waiting for transfers between devices, local(): lax.psum_scatter(jnp.concatenate([contract_tokens(gate_grad, tok_cols), c...  198 us
    dot_general x3, matrix products, contract_tokens(): lax.dot_general(left, right, (((0,), (0,)), ((), ())), preferred_element_...  74.6 us
    all_gather x1, waiting for transfers between devices, local(): lax.all_gather(cotangent, 'col', axis=0, tiled=True)  35.9 us
    convert_element_type x1, other arithmetic, local_grads(): up_grad = (hidden_grad * gate_value * sigmoid_gate).astype(jnp.bfloat16)  31.7 us
  transfers between devices with their start and end apart: 8, of which 8 were waited for; matrix products, arithmetic and copies ran while one was open for 16% of the time, Pallas kernels for 0%

commit v1 on v0

--- a/solution.py
+++ b/solution.py
@@ -2,6 +2,12 @@
 import jax.numpy as jnp
 from jax import lax
 from jax.sharding import PartitionSpec as P
+
+
+def gather_and_add(shard, name):
+    shards = lax.all_gather(shard, name, axis=0, tiled=False)
+    summed = shards.sum(axis=0)
+    return summed
 
 
 def contract_tokens(left, right):
@@ -28,7 +34,7 @@
         lax.all_gather(cotangent, "col", axis=0, tiled=True),
     )
     partial_grad = jnp.dot(cot_cols, w_down, preferred_element_type=jnp.float32)
-    hidden_grad = lax.psum(partial_grad.astype(jnp.bfloat16), "row").astype(jnp.float32)
+    hidden_grad = gather_and_add(partial_grad.astype(jnp.bfloat16), "row").astype(jnp.float32)
     gate_all, up_all = (
         lax.all_gather(gate_pre, "row", axis=0, tiled=True),
         lax.all_gather(up_pre, "row", axis=0, tiled=True),

time: 1440 us -> 1920 us (1.33)
  waiting for transfers between devices: 1200 us -> 1630 us
  other arithmetic: 53.2 us -> 81.7 us
    all_gather x0 -> x1, waiting for transfers between devices: none -> 932 us  [gather_and_add(): shards = lax.all_gather(shard, name, axis=0, tiled=False)]
    psum x1 -> x0, waiting for transfers between devices: 467 us -> none  [local(): lax.psum(partial_grad.astype(jnp.bfloat16), 'row').astype(jnp.float32)]
    reduce_scatter x1, waiting for transfers between devices: 198 us -> 167 us  [local(): lax.psum_scatter(jnp.concatenate([contract_tokens(gate_grad, tok_cols), c...]
    reduce_sum x0 -> x1, other arithmetic: none -> 28.2 us  [gather_and_add(): summed = shards.sum(axis=0)]
  transfers between devices with their start and end apart: 8 -> 8, of which waited for: 8 -> 6; matrix products, arithmetic and copies ran while one was open for 16% -> 14% of each run, Pallas kernels for 0% -> 0%
where the time goes in v1:
time: 1920 us
  waiting for transfers between devices  1630 us (85%)
  matrix products  145 us (8%)
  other arithmetic  81.7 us (4%)
  local copies, waits for them, and re-layouts  33.2 us (2%)
    all_gather x1, waiting for transfers between devices, gather_and_add(): shards = lax.all_gather(shard, name, axis=0, tiled=False)  932 us
    all_gather x1, waiting for transfers between devices, local(): lax.all_gather(up_pre, 'row', axis=0, tiled=True)  252 us
    all_gather x1, waiting for transfers between devices, local(): lax.all_gather(gate_pre, 'row', axis=0, tiled=True)  231 us
    reduce_scatter x1, waiting for transfers between devices, local(): lax.psum_scatter(jnp.concatenate([contract_tokens(gate_grad, tok_cols), c...  167 us
    dot_general x3, matrix products, contract_tokens(): lax.dot_general(left, right, (((0,), (0,)), ((), ())), preferred_element_...  78.5 us
  transfers between devices with their start and end apart: 8, of which 6 were waited for; matrix products, arithmetic and copies ran while one was open for 14% of the time, Pallas kernels for 0%

profile of v1, /device:TPU:0, one launch (start us, length us, event | category | flops | bytes accessed | tf_op | source)
XLA Modules:
  0.0 1916.6 jit_solution(2259307189308910332)
XLA Ops:
  7.2 0.7 all-gather.7.cloned.1.call-update
  7.9 0.7 all-gather.11.cloned.1.call-update
  8.7 0.7 all-gather.9.cloned.1.call-update
  9.4 35.9 %all-gather.7.cloned.1.call-done = bf16[1024,1024]{1,0:T(8,128)(2,1)} async-done(((bf16[512,1024]{1,0:T(8,128)(2,1)}), bf16[1024,1024]{1,0:T(8,128)(2,1)}) %all-gather.7.cloned.1.call-update) | async-done | bytes 2097168 | tf_op jit(solution)/shard_map/all_gather | solution.py:34
  45.4 22.3 %convolution_convert_fusion.2 = bf16[1024,7168]{1,0:T(8,128)(2,1)} fusion(bf16[1024,1024]{1,0:T(8,128)(2,1)} %all-gather.7.cloned.1.call-done, bf16[1024,7168]{1,0:T(8,128)(2,1)} %param.13), kind=kOutput, calls=%fused_computation.21 | convolution fusion | flops 15039725568 | bytes 31457280 | tf_op jit(solution)/shard_map/dot_general | solution.py:36
  67.7 0.5 all-gather.13.cloned.1.call-update
  68.3 231.1 %all-gather.11.cloned.1.call-done = bf16[1024,7168]{1,0:T(8,128)(2,1)} async-done(((bf16[256,7168]{1,0:T(8,128)(2,1)}), bf16[1024,7168]{1,0:T(8,128)(2,1)}) %all-gather.11.cloned.1.call-update) | async-done | bytes 14680080 | tf_op jit(solution)/shard_map/all_gather | solution.py:39
  299.4 252.3 %all-gather.9.cloned.1.call-done = bf16[1024,7168]{1,0:T(8,128)(2,1)} async-done(((bf16[256,7168]{1,0:T(8,128)(2,1)}), bf16[1024,7168]{1,0:T(8,128)(2,1)}) %all-gather.9.cloned.1.call-update) | async-done | bytes 14680080 | tf_op jit(solution)/shard_map/all_gather | solution.py:40
  551.7 29.4 %convert_bitcast_fusion = bf16[1024,7168]{0,1:T(8,128)(2,1)} fusion(bf16[1024,1024]{1,0:T(8,128)(2,1)S(1)} %copy-done, bf16[1024,7168]{1,0:T(8,128)(2,1)} %all-gather.9.cloned.1.call-done, bf16[1024,7168]{1,0:T(8,128)(2,1)} %all-gather.11.cloned.1.call-done), kind=kOutput, calls=%fused_computation.17 | convolution fusion | flops 15098445824 | bytes 46137344 | tf_op jit(solution)/shard_map/dot_general | solution.py:14
  581.1 12.7 reduce-scatter.6.cloned.1.call-start
  593.8 932.0 %all-gather.15.cloned.1.call-done = bf16[4096,7168]{1,0:T(8,128)(2,1)} async-done(((bf16[1024,7168]{1,0:T(8,128)(2,1)}), bf16[4096,7168]{1,0:T(8,128)(2,1)}) %all-gather.15.cloned.1.call-update) | async-done | bytes 58720272 | tf_op jit(solution)/shard_map/all_gather | solution.py:8
  1525.7 28.2 %reduce_sum.12 = bf16[1024,7168]{1,0:T(8,128)(2,1)} reduce(bf16[4,1024,7168]{2,1,0:T(8,128)(2,1)} %bitcast.14, bf16[]{:T(256)} %constant.1.clone.1), dimensions={0}, to_apply=%region_0.0 | reduce | flops 22020096 | bytes 73400320 | tf_op jit(solution)/shard_map/reduce_sum | solution.py:9
  1553.9 32.9 %fusion.9 = (bf16[1024,7168]{1,0:T(8,128)(2,1)}, bf16[1024,7168]{1,0:T(8,128)(2,1)}) fusion(bf16[1024,7168]{1,0:T(8,128)(2,1)} %all-gather.11.cloned.1.call-done, bf16[1024,7168]{1,0:T(8,128)(2,1)} %reduce_sum.12, bf16[1024,7168]{1,0:T(8,128)(2,1)} %all-gather.9.cloned.1.call-done), kind=kLoop, calls=%fused_computation.15 | loop fusion | flops 117440512 | bytes 73400320 | tf_op jit(solution)/shard_map/convert_element_type | solution.py:27
  1586.8 25.6 %convolution_convert_fusion = bf16[7168,1024]{0,1:T(8,128)(2,1)} fusion(bf16[1024,7168]{1,0:T(8,128)(2,1)} %get-tuple-element.8, bf16[1024,1024]{1,0:T(8,128)(2,1)} %all-gather.13.cloned.1.call-done), kind=kOutput, calls=%fused_computation.19 | convolution fusion | flops 15039725568 | bytes 31457280 | tf_op jit(solution)/shard_map/dot_general | solution.py:14
  1612.3 23.5 %convolution_convert_fusion.1 = bf16[7168,1024]{0,1:T(8,128)(2,1)} fusion(bf16[1024,7168]{1,0:T(8,128)(2,1)} %get-tuple-element.9, bf16[1024,1024]{1,0:T(8,128)(2,1)S(1)} %copy-done.1), kind=kOutput, calls=%fused_computation.20 | convolution fusion | flops 15039725568 | bytes 31457280 | tf_op jit(solution)/shard_map/dot_general | solution.py:14
  1635.9 20.6 %pad_maximum_fusion = bf16[7168,2048]{0,1:T(8,128)(2,1)} fusion(bf16[7168,1024]{0,1:T(8,128)(2,1)} %convolution_convert_fusion, bf16[7168,1024]{0,1:T(8,128)(2,1)} %convolution_convert_fusion.1), kind=kLoop, calls=%fused_computation.16 | loop fusion | flops 58720256 | bytes 58720256 | tf_op jit(solution)/shard_map/concatenate | solution.py:60
  1656.6 19.2 %fusion.16 = f32[1024,1024]{1,0:T(8,128)S(1)} fusion(bf16[1024,7168]{1,0:T(8,128)(2,1)} %get-tuple-element.9, bf16[7168,1024]{1,0:T(8,128)(2,1)} %param.11), kind=kOutput, calls=%fused_computation.25 | convolution fusion | flops 15032385536 | bytes 33554432 | tf_op jit(solution)/shard_map/dot_general | solution.py:45
  1675.8 24.9 %add_convert_fusion = bf16[1024,1024]{1,0:T(8,128)(2,1)} fusion(f32[1024,1024]{1,0:T(8,128)S(1)} %fusion.16, bf16[1024,7168]{1,0:T(8,128)(2,1)} %get-tuple-element.8, bf16[7168,1024]{1,0:T(8,128)(2,1)} %param.12), kind=kOutput, calls=%fused_computation.22 | convolution fusion | flops 15034482688 | bytes 35651584 | tf_op jit(solution)/shard_map/dot_general | solution.py:46
  1700.7 6.7 copy.13
  1707.4 167.2 %reduce-scatter.6.cloned.1.call-done = bf16[1792,2048]{0,1:T(8,128)(2,1)} async-done(((bf16[7168,2048]{0,1:T(8,128)(2,1)}), bf16[1792,2048]{0,1:T(8,128)(2,1)}) %reduce-scatter.6.cloned.1.call-update) | async-done | bytes 7340048 | tf_op jit(solution)/shard_map/reduce_scatter | solution.py:59
  1874.7 9.8 fusion.15
  1884.4 8.4 copy.11
  1892.8 8.4 copy.12
  1901.2 8.2 reduce-scatter.4.cloned.1.call-done
  (17 shorter events, 0.4 us)
Async XLA Ops:
  7.2 38.2 %all-gather.7.cloned.1.call-start = ((), (), s32[]{:S(2)}) async-start(), calls=%async_computation.3 | async-start | bytes 3145728 | tf_op jit(solution)/shard_map/all_gather | solution.py:34
  7.9 291.5 %all-gather.11.cloned.1.call-start = ((), (), s32[]{:S(2)}) async-start(), calls=%async_computation.5 | async-start | bytes 18350080 | tf_op jit(solution)/shard_map/all_gather | solution.py:39
  8.6 543.0 %all-gather.9.cloned.1.call-start = ((), (), s32[]{:S(2)}) async-start(), calls=%async_computation.4 | async-start | bytes 18350080 | tf_op jit(solution)/shard_map/all_gather | solution.py:40
  9.4 1516.4 %all-gather.15.cloned.1.call-start = ((), (), s32[]{:S(2)}) async-start(), calls=%async_computation.10 | async-start | bytes 73400320 | tf_op jit(solution)/shard_map/all_gather | solution.py:8
  67.6 484.1 %copy-start = (bf16[1024,1024]{1,0:T(8,128)(2,1)S(1)}, bf16[1024,1024]{1,0:T(8,128)(2,1)}, u32[]{:S(2)}) copy-start(bf16[1024,1024]{1,0:T(8,128)(2,1)} %all-gather.7.cloned.1.call-done) | copy-start | bytes 6291460
  67.7 1519.1 %all-gather.13.cloned.1.call-start = ((), (), s32[]{:S(2)}) async-start(), calls=%async_computation.7 | async-start | bytes 3145728 | tf_op jit(solution)/shard_map/all_gather | solution.py:33
  68.3 1632.5 %reduce-scatter.8.cloned.1.call-start = ((), (), s32[]{:S(2)}) async-start(), calls=%async_computation.9 | async-start | bytes 18350080 | tf_op jit(solution)/shard_map/reduce_scatter | solution.py:52
  581.1 1293.6 %reduce-scatter.6.cloned.1.call-start = ((), (), s32[]{:S(2)}) async-start(), calls=%async_computation.8 | async-start | bytes 36700160 | tf_op jit(solution)/shard_map/reduce_scatter | solution.py:59
  1586.8 25.6 %copy-start.1 = (bf16[1024,1024]{1,0:T(8,128)(2,1)S(1)}, bf16[1024,1024]{1,0:T(8,128)(2,1)}, u32[]{:S(2)}) copy-start(bf16[1024,1024]{1,0:T(8,128)(2,1)} %all-gather.13.cloned.1.call-done) | copy-start | bytes 6291460
  1656.5 252.9 %reduce-scatter.4.cloned.1.call-start = ((), (), s32[]{:S(2)}) async-start(), calls=%async_computation.6 | async-start | bytes 3145728 | tf_op jit(solution)/shard_map/reduce_scatter | solution.py:43
Sparse Core Ops, SparseCore 0:
  9.5 35.8 all-gather.6
  46.9 252.4 all-gather.10
  301.0 250.6 all-gather.8
  553.1 972.5 all-gather.14
  1527.1 31.2 all-gather.12
  1560.9 110.0 reduce-scatter.7
  1673.6 201.0 reduce-scatter.5
  1877.5 31.8 reduce-scatter.3
